TPU v7x, 32 devices: a whole 2x2x4 slice. The times are simulated.
32 devices in a mesh: gx: 8 (over z, x), gy: 4 (over y, core).
Axes of the slice: x: 2, y: 2, z: 4, core: 2. Of those that a mesh axis runs over, the one named last changes fastest.
Arguments:
- fields: float32 [4, 32, 32, 512], P(None, 'gx', 'gy'), may hold values from -6 to 6
- velocity: float32 [3, 32, 32, 512], P(None, 'gx', 'gy'), may hold values from -4 to 4
- diffusion: float32 [4], replicated, may hold values from 0.1 to 0.6
- panel_owner: int32 [32768, 1], P(('gx', 'gy')), may hold values from 0 to 31; in each aligned block of 1024 rows (0 to 1023, 1024 to 2047, ...) at most 128 rows name the same one
- panel_cell: int32 [32768], P(('gx', 'gy')), may hold values from 0 to 16383
- panel_bins: int32 [16, 32768], P(None, ('gx', 'gy')), may hold values from 0 to 127
- panel_position: float32 [3, 32768], P(None, ('gx', 'gy')), may hold values from -1 to 1, as said below
- panel_area: float32 [32768], P(('gx', 'gy')), may hold values from 0.3 to 3
- observer_position: float32 [3, 2048], replicated, may hold values from -2 to 2.25, as said below
Outputs:
- advanced: float32 [4, 32, 32, 512], P(None, 'gx', 'gy')
- signal: float32 [2048, 128], P(('gx', 'gy'))
Inputs may be any that keep to these rules, and one draw needn't show every extreme that they name: `panel_owner`: among the panels of one device at most 128 name the same brick, a bound that some block reaches; every brick is named somewhere. `panel_cell`: A cell of the owning brick, numbered (x * 8 + y) * 512 + z in that brick's own coordinates. `panel_position`: every panel's third coordinate is 0 or less. `observer_position`: every observer's third coordinate is 0.25 or more.
All inputs are finite; a program needn't handle non-finite values.
Results may differ from a plain program's by a relative error of at most 0.0029.
Values sent between devices are 32-bit elements; how exact they have to be, the bound alone decides.
A program may use at most 128 MiB of HBM per device.

v0:
```python
import functools

import jax
import jax.numpy as jnp
from jax import lax
from jax.experimental import pallas as pl
from jax.experimental.pallas import tpu as pltpu
from jax.sharding import PartitionSpec as P

MESH = pl.DeviceIdType.MESH
time_step = 0.15
NT = (((1,), (1,)), ((), ()))


def axis_terms(center, ahead_one, ahead_two, behind_one, behind_two):
    first = (8.0 * (ahead_one - behind_one) - (ahead_two - behind_two)) / 12.0
    second = (16.0 * (ahead_one + behind_one) - (ahead_two + behind_two) - 30.0 * center) / 12.0
    return (first, second)


def section(cells_ref, x_ref, y_ref, pad_ref, velocity_ref, diffusion_ref, write):
    quantities, nx, ny, nz = cells_ref.shape
    for c in range(quantities):
        def plane(x):
            if x < 0:
                return x_ref[0, c, 2 + x]
            if x >= nx:
                return x_ref[1, c, x - nx]
            return cells_ref[c, x]

        for x in range(nx):
            center = cells_ref[c, x]
            pad_ref[c, x, 6:8, :] = y_ref[0, c, x]
            pad_ref[c, x, 8:8 + ny, :] = center
            pad_ref[c, x, 8 + ny:10 + ny, :] = y_ref[1, c, x]

            def along_y(k):
                return pad_ref[c, x, 8 + k:8 + k + ny, :]

            first_x, second_x = axis_terms(
                center, plane(x + 1), plane(x + 2), plane(x - 1), plane(x - 2))
            first_y, second_y = axis_terms(
                center, along_y(1), along_y(2), along_y(-1), along_y(-2))
            first_z, second_z = axis_terms(
                center, pltpu.roll(center, nz - 1, 1), pltpu.roll(center, nz - 2, 1),
                pltpu.roll(center, 1, 1), pltpu.roll(center, 2, 1))
            advect = (
                velocity_ref[0, x] * first_x + velocity_ref[1, x] * first_y
                + velocity_ref[2, x] * first_z)
            write(c, x, center, -advect + diffusion_ref[c] * (second_x + second_y + second_z))


def two_parts(values, axis):
    high = values.astype(jnp.bfloat16)
    low = (values - high.astype(jnp.float32)).astype(jnp.bfloat16)
    return jnp.concatenate([high, low], axis=axis)


def emission_kernel(
    grid_x, grid_y, cap, scale, tile,
    fields_in, velocity_in, diffusion_ref, owner_in, cell_in, bins_in, position_in, area_in, observer_in,
    advanced_ref, signal_ref,
    fields_ref, velocity_ref, owner_ref, cell_ref, bins_ref, position_ref, area_ref, observer_ref,
    middle_ref, pad_ref, x_one_ref, x_two_ref, y_one_ref, y_two_ref, y_out_one_ref, y_out_two_ref,
    request_ref, arrived_ref, looked_ref, returned_ref, table_ref, rows_ref, total_ref, pair_ref, merged_ref, landed_ref,
    request_send, request_recv, sample_send, sample_recv, total_send, total_recv,
    halo_send, halo_recv, pair_send, pair_recv, load_sem,
):
    devices = grid_x * grid_y
    my_x, my_y = lax.axis_index("gx"), lax.axis_index("gy")
    me = my_x * grid_y + my_y
    nx, ny = fields_ref.shape[1:3]
    panels = owner_ref.shape[1]
    blocks, bins = bins_ref.shape[0], signal_ref.shape[1]
    observers = observer_ref.shape[1]
    width = observers // blocks
    share = observers // devices
    per_block = width // share
    quantities = fields_ref.shape[0]
    rows = fields_ref.shape[1] * fields_ref.shape[2]
    depth = fields_ref.shape[3]
    chunks = depth // 128
    row_shift = (depth - 1).bit_length()

    def at(d):
        return (d // grid_y, lax.rem(d, grid_y))

    def request_copy(mine, other, slot_here, slot_there):
        return pltpu.make_async_remote_copy(
            src_ref=request_ref.at[mine], dst_ref=arrived_ref.at[slot_there],
            send_sem=request_send.at[mine], recv_sem=request_recv.at[slot_there],
            device_id=at(other), device_id_type=MESH)

    def sample_copy(mine, other, slot_there):
        return pltpu.make_async_remote_copy(
            src_ref=looked_ref.at[mine], dst_ref=returned_ref.at[slot_there],
            send_sem=sample_send.at[mine], recv_sem=sample_recv.at[slot_there],
            device_id=at(other), device_id_type=MESH)

    core = lax.rem(my_y, 2)
    half = per_block // 2
    mine = me // 2

    def pair_copy(h):
        return pltpu.make_async_remote_copy(
            src_ref=total_ref.at[2 * h + 1 - core], dst_ref=pair_ref.at[h],
            send_sem=pair_send.at[h], recv_sem=pair_recv.at[h],
            device_id=(my_x, my_y + 1 - 2 * core), device_id_type=MESH)

    def total_copy(h, slot_there):
        return pltpu.make_async_remote_copy(
            src_ref=merged_ref.at[h], dst_ref=landed_ref.at[slot_there],
            send_sem=total_send.at[h], recv_sem=total_recv.at[slot_there],
            device_id=at(2 * h + core), device_id_type=MESH)

    def merge(block):
        for r in range(half):
            h = block * half + r
            pair_copy(h).wait_recv()
            merged_ref[h] = total_ref[2 * h + core] + pair_ref[h]

            @pl.when(h != mine)
            def _():
                total_copy(h, mine).start()

    loads = [
        pltpu.make_async_copy(source, target, load_sem.at[i])
        for i, (source, target) in enumerate([
            (owner_in, owner_ref), (cell_in, cell_ref), (fields_in, fields_ref),
            (velocity_in, velocity_ref), (area_in, area_ref), (bins_in, bins_ref),
            (position_in, position_ref), (observer_in, observer_ref)])
    ]
    for load in loads:
        load.start()

    def halo_copies(stage, cells_ref, x_ref, y_out_ref, y_ref):
        def copy(k, source, target, where):
            return pltpu.make_async_remote_copy(
                src_ref=source, dst_ref=target, send_sem=halo_send.at[4 * stage + k],
                recv_sem=halo_recv.at[4 * stage + k], device_id=where, device_id_type=MESH)

        up_x, down_x = lax.rem(my_x + 1, grid_x), lax.rem(my_x + grid_x - 1, grid_x)
        up_y, down_y = lax.rem(my_y + 1, grid_y), lax.rem(my_y + grid_y - 1, grid_y)
        return [
            copy(0, cells_ref.at[:, nx - 2:nx], x_ref.at[0], (up_x, my_y)),
            copy(1, cells_ref.at[:, 0:2], x_ref.at[1], (down_x, my_y)),
            copy(2, y_out_ref.at[1], y_ref.at[0], (my_x, up_y)),
            copy(3, y_out_ref.at[0], y_ref.at[1], (my_x, down_y)),
        ]

    halo_one = halo_copies(0, fields_ref, x_one_ref, y_out_one_ref, y_one_ref)
    halo_two = halo_copies(1, middle_ref, x_two_ref, y_out_two_ref, y_two_ref)

    barrier = pltpu.get_barrier_semaphore()

    @pl.loop(1, devices)
    def _(k):
        pl.semaphore_signal(
            barrier, inc=1, device_id=at(lax.rem(me + k, devices)), device_id_type=MESH)

    loads[0].wait()
    loads[1].wait()

    owner = owner_ref[...]
    cell = cell_ref[...]
    owned = (lax.broadcasted_iota(jnp.int32, (devices, panels), 0) == owner)
    owned_f = owned.astype(jnp.float32)
    owned_b = owned_f.astype(jnp.bfloat16)
    earlier = (
        lax.broadcasted_iota(jnp.int32, (128, 128), 0)
        < lax.broadcasted_iota(jnp.int32, (128, 128), 1)
    ).astype(jnp.float32).astype(jnp.bfloat16)
    running = jnp.zeros((devices, 1), jnp.float32)
    ranks = []
    for j in range(panels // 128):
        part = slice(j * 128, (j + 1) * 128)
        before = jnp.dot(owned_b[:, part], earlier, preferred_element_type=jnp.float32) + running
        ranks.append(jnp.sum(owned_f[:, part] * before, axis=0, keepdims=True))
        running = running + jnp.sum(owned_f[:, part], axis=1, keepdims=True)
    rank = jnp.concatenate(ranks, axis=1).astype(jnp.int32)
    ranked = (lax.broadcasted_iota(jnp.int32, (cap, panels), 0) == rank).astype(jnp.float32)
    ranked_b = ranked.astype(jnp.bfloat16)
    cell_high = lax.shift_right_logical(cell, 7).astype(jnp.float32)
    cell_low = lax.bitwise_and(cell, 127).astype(jnp.float32)
    both = jnp.concatenate([owned_f * cell_high, owned_f * cell_low], axis=0).astype(jnp.bfloat16)
    packed = lax.dot_general(both, ranked_b, NT, preferred_element_type=jnp.float32)
    wanted = (packed[:devices] * 128.0 + packed[devices:]).astype(jnp.int32)
    for d in range(devices):
        request_ref[d] = wanted[d:d + 1]

    loads[2].wait()
    y_out_one_ref[0] = fields_ref[:, :, 0:2, :]
    y_out_one_ref[1] = fields_ref[:, :, ny - 2:ny, :]
    pl.semaphore_wait(barrier, devices - 1)

    @pl.loop(1, devices)
    def _(k):
        other = lax.rem(me + k, devices)
        request_copy(other, other, me, me).start()

    arrived_ref[me] = request_ref[me]
    for copy in halo_one:
        copy.start()

    for c in range(quantities):
        plane = fields_ref[c].reshape(rows, depth)
        stacked = jnp.concatenate([plane[:, i * 128:(i + 1) * 128] for i in range(chunks)], axis=0)
        table_ref[c * 128:(c + 1) * 128, :] = two_parts(stacked.T, 1)

    def receive_request(s):
        @pl.when(s != me)
        def _():
            request_copy(s, s, me, s).wait_recv()

    @pl.loop(0, devices // 2)
    def _(pair):
        first = lax.rem(me + devices - 2 * pair, devices)
        second = lax.rem(me + devices - 2 * pair - 1, devices)
        receive_request(first)
        receive_request(second)
        asked = jnp.concatenate([arrived_ref[first], arrived_ref[second]], axis=1)
        low = lax.bitwise_and(asked, 127)
        line = lax.shift_right_logical(asked, row_shift)
        chunk = lax.bitwise_and(lax.shift_right_logical(asked, 7), chunks - 1)
        high = chunk * rows + line
        pick = (
            lax.broadcasted_iota(jnp.int32, (chunks * rows, 2 * cap), 0) == high
        ).astype(jnp.float32).astype(jnp.bfloat16)
        found = jnp.dot(
            table_ref[...], jnp.concatenate([pick, pick], axis=0),
            preferred_element_type=jnp.float32)
        lane = lax.broadcasted_iota(jnp.int32, (128, 2 * cap), 0) == low
        values = jnp.concatenate(
            [
                jnp.sum(jnp.where(lane, found[c * 128:(c + 1) * 128], 0.0), axis=0, keepdims=True)
                for c in range(quantities)
            ],
            axis=0,
        )
        looked_ref[first] = values[:, :cap]
        looked_ref[second] = values[:, cap:]

        @pl.when(first != me)
        def _():
            sample_copy(first, first, me).start()

        sample_copy(second, second, me).start()

    returned_ref[me] = looked_ref[me]

    for load in loads[3:]:
        load.wait()
    for copy in halo_one:
        copy.wait_recv()

    def keep_middle(c, x, center, rate):
        value = center + time_step * rate
        middle_ref[c, x] = value
        y_out_two_ref[0, c, x] = value[0:2]
        y_out_two_ref[1, c, x] = value[ny - 2:ny]

    section(fields_ref, x_one_ref, y_one_ref, pad_ref, velocity_ref, diffusion_ref, keep_middle)
    for copy in halo_two:
        copy.start()

    @pl.loop(1, devices)
    def _(k):
        s = lax.rem(me + devices - k, devices)
        sample_copy(s, s, s).wait_recv()

    weight = scale * area_ref[...]
    for c in range(quantities):
        got = returned_ref[:, c, :].T
        spread = jnp.dot(
            two_parts(got, 1), jnp.concatenate([owned_b, owned_b], axis=0),
            preferred_element_type=jnp.float32)
        sample = jnp.sum(spread * ranked, axis=0, keepdims=True)
        rows_ref[c:c + 1, :] = sample * weight

    home = me // per_block
    lag = min(3, blocks)

    @pl.loop(0, blocks)
    def _(turn):
        block = lax.rem(home + 1 + turn, blocks)
        place = pl.multiple_of(block * width, width)
        spots = [
            jnp.broadcast_to(observer_ref[k:k + 1, pl.ds(place, width)], (128, width)).T
            for k in range(3)
        ]
        line = bins_ref[pl.ds(block, 1), :]
        acc = jnp.zeros((width, bins), jnp.float32)
        for j in range(panels // tile):
            pieces = []
            for i in range(width // 32):
                strip = []
                for h in range(tile // 128):
                    lanes = slice(j * tile + h * 128, j * tile + (h + 1) * 128)
                    take = slice(i * 32, (i + 1) * 32)
                    d0 = spots[0][take] - position_ref[0:1, lanes]
                    d1 = spots[1][take] - position_ref[1:2, lanes]
                    d2 = spots[2][take] - position_ref[2:3, lanes]
                    inverse = lax.rsqrt(d0 * d0 + d1 * d1 + d2 * d2)
                    along = (
                        rows_ref[1:2, lanes] * d0
                        + rows_ref[2:3, lanes] * d1
                        + rows_ref[3:4, lanes] * d2
                    )
                    strip.append(
                        ((rows_ref[0:1, lanes] + along * inverse) * inverse).astype(jnp.bfloat16))
                pieces.append(jnp.concatenate(strip, axis=1))
            emitted = jnp.concatenate(pieces, axis=0)
            onehot = (
                lax.broadcasted_iota(jnp.int32, (bins, tile), 0) == line[:, j * tile:(j + 1) * tile]
            ).astype(jnp.float32).astype(jnp.bfloat16)
            acc = acc + lax.dot_general(emitted, onehot, NT, preferred_element_type=jnp.float32)
        for q in range(per_block):
            total_ref[block * per_block + q] = acc[q * share:(q + 1) * share]
        for r in range(half):
            pair_copy(block * half + r).start()

        @pl.when(turn >= lag)
        def _():
            merge(lax.rem(home + 1 + turn - lag + blocks, blocks))

    for back in reversed(range(lag)):
        merge(lax.rem(home - back + blocks, blocks))
    landed_ref[mine] = merged_ref[mine]

    for copy in halo_two:
        copy.wait_recv()

    def keep_advanced(c, x, center, rate):
        advanced_ref[c, x] = 0.5 * fields_ref[c, x] + 0.5 * (center + time_step * rate)

    section(middle_ref, x_two_ref, y_two_ref, pad_ref, velocity_ref, diffusion_ref, keep_advanced)

    @pl.loop(1, devices // 2)
    def _(k):
        s = lax.rem(mine + devices // 2 - k, devices // 2)
        total_copy(s, s).wait_recv()

    signal_ref[...] = jnp.sum(landed_ref[...], axis=0)

    @pl.loop(1, devices)
    def _(k):
        other = lax.rem(me + k, devices)
        request_copy(other, other, me, me).wait_send()
        sample_copy(other, other, me).wait_send()

    @pl.loop(1, devices // 2)
    def _(k):
        total_copy(lax.rem(mine + k, devices // 2), mine).wait_send()

    @pl.loop(0, devices // 2)
    def _(h):
        pair_copy(h).wait_send()

    for copy in halo_one + halo_two:
        copy.wait_send()


def per_device(
    bins, fields, velocity, diffusion, panel_owner, panel_cell, panel_bins,
    panel_position, panel_area, observer_position,
):
    grid_x = lax.axis_size("gx")
    grid_y = lax.axis_size("gy")
    devices = grid_x * grid_y
    panels = panel_cell.shape[0]
    cap = 4 * panels // devices
    observers = observer_position.shape[1]
    share = observers // devices
    quantities = fields.shape[0]
    scale = (bins / (panels * devices)) ** 0.5
    columns = 2 * fields.shape[1] * fields.shape[2] * fields.shape[3] // 128

    owner, cell, area = (
        panel_owner.reshape(1, panels), panel_cell.reshape(1, panels), panel_area.reshape(1, panels))
    vmem = pl.BlockSpec(memory_space=pltpu.VMEM)
    smem = pl.BlockSpec(memory_space=pltpu.SMEM)
    anywhere = pl.BlockSpec(memory_space=pl.ANY)
    nx, ny, nz = fields.shape[1:]
    beside_x = pltpu.VMEM((2, quantities, 2, ny, nz), jnp.float32)
    beside_y = pltpu.VMEM((2, quantities, nx, 2, nz), jnp.float32)
    return pl.pallas_call(
        functools.partial(emission_kernel, grid_x, grid_y, cap, scale, min(256, panels)),
        out_shape=(
            jax.ShapeDtypeStruct(fields.shape, jnp.float32),
            jax.ShapeDtypeStruct((share, bins), jnp.float32),
        ),
        in_specs=[anywhere] * 2 + [smem] + [anywhere] * 6,
        out_specs=(vmem, vmem),
        scratch_shapes=[
            pltpu.VMEM(array.shape, array.dtype)
            for array in (
                fields, velocity, owner, cell, panel_bins, panel_position, area, observer_position)
        ] + [
            pltpu.VMEM(fields.shape, jnp.float32),
            pltpu.VMEM((quantities, nx, ny + 16, nz), jnp.float32),
            beside_x, beside_x, beside_y, beside_y, beside_y, beside_y,
            pltpu.VMEM((devices, 1, cap), jnp.int32),
            pltpu.VMEM((devices, 1, cap), jnp.int32),
            pltpu.VMEM((devices, quantities, cap), jnp.float32),
            pltpu.VMEM((devices, quantities, cap), jnp.float32),
            pltpu.VMEM((quantities * 128, columns), jnp.bfloat16),
            pltpu.VMEM((quantities, panels), jnp.float32),
            pltpu.VMEM((devices, share, bins), jnp.float32),
            pltpu.VMEM((devices // 2, share, bins), jnp.float32),
            pltpu.VMEM((devices // 2, share, bins), jnp.float32),
            pltpu.VMEM((devices // 2, share, bins), jnp.float32),
        ] + [
            pltpu.SemaphoreType.DMA((devices,))] * 4 + [
            pltpu.SemaphoreType.DMA((devices // 2,))] * 2 + [
            pltpu.SemaphoreType.DMA((8,))] * 2 + [
            pltpu.SemaphoreType.DMA((devices // 2,))] * 2 + [
            pltpu.SemaphoreType.DMA((8,))],
        compiler_params=pltpu.CompilerParams(
            collective_id=0, has_side_effects=True),
        cost_estimate=pl.CostEstimate(
            flops=40 * 10**9, bytes_accessed=4 * 10**6, transcendentals=2 * 10**6),
    )(fields, velocity, diffusion, owner, cell, panel_bins, panel_position, area, observer_position)


def solution(mesh):
    in_specs = (
        P(None, "gx", "gy", None),
        P(None, "gx", "gy", None),
        P(),
        P(("gx", "gy"), None),
        P(("gx", "gy")),
        P(None, ("gx", "gy")),
        P(None, ("gx", "gy")),
        P(("gx", "gy")),
        P(),
    )
    out_specs = (P(None, "gx", "gy", None), P(("gx", "gy"), None))
    return jax.shard_map(
        functools.partial(per_device, 128),
        mesh=mesh, in_specs=in_specs, out_specs=out_specs, check_vma=False,
    )
```

profile of v0, /device:TPU:15, one launch (start us, length us, event | category | flops | bytes accessed | tf_op | source)
XLA Modules:
  0.0 42.8 jit_solution(3374696847825723214)
XLA Ops:
  0.6 39.8 %shard_map.104 = (f32[4,4,8,512]{3,2,1,0:T(8,128)}, f32[64,128]{1,0:T(8,128)}) custom-call(f32[4,4,8,512]{3,2,1,0:T(8,128)} %fields_in.1, f32[3,4,8,512]{3,2,1,0:T(8,128)} %velocity_in.1, f32[4]{0:T(128)} %diffusion_ref.1, s32[1,1024]{1,0:T(1,128)} %bitcast.3, s32[1,1024]{1,0:T(1,128)} %bitcast.4, s32[16,1024]{1,0:T(8,128)} %bins_in.1, ...), custom_call_target="tpu_custom_call" | custom-call | flops 40000000000 | bytes 4000000 | tf_op jit(solution)/shard_map/pallas_call | solution.py:386
  40.5 0.0 copy-start
  40.5 1.7 %copy.13 = f32[4,4,8,512]{3,2,1,0:T(8,128)} copy(f32[4,4,8,512]{3,2,1,0:T(8,128)} %get-tuple-element.4) | data formatting | bytes 524288
  42.1 0.0 copy-done
  42.1 0.6 %copy.14 = f32[64,128]{1,0:T(8,128)} copy(f32[64,128]{1,0:T(8,128)S(1)} %copy-done) | data formatting | bytes 65536
Async XLA Ops:
  40.5 1.7 %copy-start = (f32[64,128]{1,0:T(8,128)S(1)}, f32[64,128]{1,0:T(8,128)}, u32[]{:S(2)}) copy-start(f32[64,128]{1,0:T(8,128)} %get-tuple-element.5) | copy-start | bytes 98308
where the time goes:
time: 43 us; the launch traced here: 42.8 us
  Pallas kernels  39.8 us (93%)
  local copies, waits for them, and re-layouts  2.3 us (5%)
  between operations  0.65 us (2%)
    pallas_call x1, Pallas kernels, per_device(): pl.pallas_call(functools.partial(emission_kernel, grid_x, grid_y, cap, sc...  39.8 us
    unnamed x4, local copies, waits for them, and re-layouts  2.3 us

commit v1 on v0

--- a/solution.py
+++ b/solution.py
@@ -56,15 +56,36 @@
     return jnp.concatenate([high, low], axis=axis)
 
 
+def three_parts(values):
+    high = values.astype(jnp.bfloat16).astype(jnp.float32)
+    rest = values - high
+    middle = rest.astype(jnp.bfloat16).astype(jnp.float32)
+    return high, middle, rest - middle
+
+
+def observer_side(values, width):
+    high, middle, low = three_parts(values)
+    pieces = [high, middle, low, high, middle, high]
+    used = len(pieces) * values.shape[0]
+    filled = jnp.concatenate(pieces + [jnp.zeros((128 - used, width), jnp.float32)], axis=0)
+    return filled.T.astype(jnp.bfloat16)
+
+
+def panel_side(values):
+    high, middle, low = three_parts(values)
+    return jnp.concatenate([high, high, high, middle, middle, low], axis=0).astype(jnp.bfloat16)
+
+
 def emission_kernel(
     grid_x, grid_y, cap, scale, tile,
-    fields_in, velocity_in, diffusion_ref, owner_in, cell_in, bins_in, position_in, area_in, observer_in,
+    fields_in, velocity_in, diffusion_in, owner_in, cell_in, bins_in, position_in, area_in, observer_in,
     advanced_ref, signal_ref,
-    fields_ref, velocity_ref, owner_ref, cell_ref, bins_ref, position_ref, area_ref, observer_ref,
+    fields_ref, velocity_ref, diffusion_ref, owner_ref, cell_ref, bins_ref, position_ref, area_ref, observer_ref,
     middle_ref, pad_ref, x_one_ref, x_two_ref, y_one_ref, y_two_ref, y_out_one_ref, y_out_two_ref,
-    request_ref, arrived_ref, looked_ref, returned_ref, table_ref, rows_ref, total_ref, pair_ref, merged_ref, landed_ref,
+    request_ref, arrived_ref, looked_ref, returned_ref, table_ref, ranked_ref,
+    place_ref, lines_out_ref, lines_ref, weighted_ref, near_ref, toward_ref, inverse_ref, hot_ref, sum_ref, landed_ref,
     request_send, request_recv, sample_send, sample_recv, total_send, total_recv,
-    halo_send, halo_recv, pair_send, pair_recv, load_sem,
+    halo_send, halo_recv, place_send, place_recv, lines_send, lines_recv, weighted_send, weighted_recv, load_sem,
 ):
     devices = grid_x * grid_y
     my_x, my_y = lax.axis_index("gx"), lax.axis_index("gy")
@@ -82,8 +103,47 @@
     chunks = depth // 128
     row_shift = (depth - 1).bit_length()
 
+    members = 2 * grid_y
+    groups = devices // members
+    own_blocks = blocks // members
+    across = grid_y // 2
+    my_bit = lax.rem(my_x // 2, 2)
+    my_member = my_bit * grid_y + my_y
+    my_group = (my_x // 4) * 2 + lax.rem(my_x, 2)
+
     def at(d):
         return (d // grid_y, lax.rem(d, grid_y))
+
+    def member_at(group, member):
+        x = (group // 2) * 4 + (member // grid_y) * 2 + lax.rem(group, 2)
+        return (x, lax.rem(member, grid_y))
+
+    def block_of(member, i):
+        bit, y = member // grid_y, member % grid_y
+        return ((y % 2) * 2 + bit) * (own_blocks * across) + i * across + y // 2
+
+    def member_of(block):
+        y = lax.rem(block, across)
+        bit = lax.rem(block // (across * own_blocks), 2)
+        core = block // (across * own_blocks * 2)
+        return bit * grid_y + y * 2 + core
+
+    barrier = pltpu.get_barrier_semaphore()
+
+    @pl.loop(1, devices)
+    def _(k):
+        pl.semaphore_signal(
+            barrier, inc=1, device_id=at(lax.rem(me + k, devices)), device_id_type=MESH)
+
+    loads = [
+        pltpu.make_async_copy(source, target, load_sem.at[i])
+        for i, (source, target) in enumerate([
+            (owner_in, owner_ref), (cell_in, cell_ref), (fields_in, fields_ref),
+            (position_in, position_ref), (bins_in, bins_ref), (observer_in, observer_ref),
+            (area_in, area_ref), (velocity_in, velocity_ref), (diffusion_in, diffusion_ref)])
+    ]
+    for load in loads:
+        load.start()
 
     def request_copy(mine, other, slot_here, slot_there):
         return pltpu.make_async_remote_copy(
@@ -97,41 +157,30 @@
             send_sem=sample_send.at[mine], recv_sem=sample_recv.at[slot_there],
             device_id=at(other), device_id_type=MESH)
 
-    core = lax.rem(my_y, 2)
-    half = per_block // 2
-    mine = me // 2
-
-    def pair_copy(h):
+    def mate_copy(source, target, send, recv, other):
         return pltpu.make_async_remote_copy(
-            src_ref=total_ref.at[2 * h + 1 - core], dst_ref=pair_ref.at[h],
-            send_sem=pair_send.at[h], recv_sem=pair_recv.at[h],
-            device_id=(my_x, my_y + 1 - 2 * core), device_id_type=MESH)
-
-    def total_copy(h, slot_there):
+            src_ref=source, dst_ref=target, send_sem=send, recv_sem=recv,
+            device_id=member_at(my_group, other), device_id_type=MESH)
+
+    def place_copy(other, slot):
+        return mate_copy(
+            place_ref.at[slot, 0:4], place_ref.at[slot, 0:4],
+            place_send.at[other], place_recv.at[slot], other)
+
+    def lines_copy(other, slot):
+        return mate_copy(
+            lines_out_ref.at[other], lines_ref.at[slot], lines_send.at[other], lines_recv.at[slot], other)
+
+    def weighted_copy(other, slot):
+        return mate_copy(
+            weighted_ref.at[slot, 0:4], weighted_ref.at[slot, 0:4],
+            weighted_send.at[other], weighted_recv.at[slot], other)
+
+    def total_copy(i, k, other, slot):
         return pltpu.make_async_remote_copy(
-            src_ref=merged_ref.at[h], dst_ref=landed_ref.at[slot_there],
-            send_sem=total_send.at[h], recv_sem=total_recv.at[slot_there],
-            device_id=at(2 * h + core), device_id_type=MESH)
-
-    def merge(block):
-        for r in range(half):
-            h = block * half + r
-            pair_copy(h).wait_recv()
-            merged_ref[h] = total_ref[2 * h + core] + pair_ref[h]
-
-            @pl.when(h != mine)
-            def _():
-                total_copy(h, mine).start()
-
-    loads = [
-        pltpu.make_async_copy(source, target, load_sem.at[i])
-        for i, (source, target) in enumerate([
-            (owner_in, owner_ref), (cell_in, cell_ref), (fields_in, fields_ref),
-            (velocity_in, velocity_ref), (area_in, area_ref), (bins_in, bins_ref),
-            (position_in, position_ref), (observer_in, observer_ref)])
-    ]
-    for load in loads:
-        load.start()
+            src_ref=sum_ref.at[i, k * share:(k + 1) * share], dst_ref=landed_ref.at[slot],
+            send_sem=total_send.at[i * per_block + k], recv_sem=total_recv.at[slot],
+            device_id=at(other), device_id_type=MESH)
 
     def halo_copies(stage, cells_ref, x_ref, y_out_ref, y_ref):
         def copy(k, source, target, where):
@@ -150,13 +199,6 @@
 
     halo_one = halo_copies(0, fields_ref, x_one_ref, y_out_one_ref, y_one_ref)
     halo_two = halo_copies(1, middle_ref, x_two_ref, y_out_two_ref, y_two_ref)
-
-    barrier = pltpu.get_barrier_semaphore()
-
-    @pl.loop(1, devices)
-    def _(k):
-        pl.semaphore_signal(
-            barrier, inc=1, device_id=at(lax.rem(me + k, devices)), device_id_type=MESH)
 
     loads[0].wait()
     loads[1].wait()
@@ -178,8 +220,11 @@
         ranks.append(jnp.sum(owned_f[:, part] * before, axis=0, keepdims=True))
         running = running + jnp.sum(owned_f[:, part], axis=1, keepdims=True)
     rank = jnp.concatenate(ranks, axis=1).astype(jnp.int32)
-    ranked = (lax.broadcasted_iota(jnp.int32, (cap, panels), 0) == rank).astype(jnp.float32)
-    ranked_b = ranked.astype(jnp.bfloat16)
+    ranked_b = (
+        lax.broadcasted_iota(jnp.int32, (cap, panels), 0) == rank
+    ).astype(jnp.float32).astype(jnp.bfloat16)
+    ranked_ref[0:cap] = ranked_b
+    ranked_ref[cap:2 * cap] = ranked_b
     cell_high = lax.shift_right_logical(cell, 7).astype(jnp.float32)
     cell_low = lax.bitwise_and(cell, 127).astype(jnp.float32)
     both = jnp.concatenate([owned_f * cell_high, owned_f * cell_low], axis=0).astype(jnp.bfloat16)
@@ -191,21 +236,72 @@
     loads[2].wait()
     y_out_one_ref[0] = fields_ref[:, :, 0:2, :]
     y_out_one_ref[1] = fields_ref[:, :, ny - 2:ny, :]
-    pl.semaphore_wait(barrier, devices - 1)
-
-    @pl.loop(1, devices)
-    def _(k):
-        other = lax.rem(me + k, devices)
-        request_copy(other, other, me, me).start()
-
-    arrived_ref[me] = request_ref[me]
-    for copy in halo_one:
-        copy.start()
+    loads[3].wait()
+    position = position_ref[...]
+    place_ref[my_member, 0:1] = jnp.sum(position * position, axis=0, keepdims=True)
+    place_ref[my_member, 1:4] = position
+    place_ref[:, 4:5] = jnp.ones((members, 1, panels), jnp.float32)
+    place_ref[:, 5:8] = jnp.zeros((members, 3, panels), jnp.float32)
+    loads[4].wait()
+    for j in range(members):
+        for i in range(own_blocks):
+            b = block_of(j, i)
+            lines_out_ref[j, i:i + 1] = bins_ref[b:b + 1]
+    lines_ref[my_member] = lines_out_ref[my_member]
+
+    loads[5].wait()
+    line8 = lax.broadcasted_iota(jnp.int32, (8, width), 0)
+    for i in range(own_blocks):
+        spot = pl.multiple_of(block_of(my_member, i) * width, width)
+        o0, o1, o2 = [observer_ref[k:k + 1, pl.ds(spot, width)] for k in range(3)]
+        square = o0 * o0 + o1 * o1 + o2 * o2
+        near = jnp.where(line8 == 0, 1.0, 0.0)
+        toward = jnp.where(line8 >= 5, -1.0, 0.0)
+        for k, line in enumerate((o0, o1, o2)):
+            near = jnp.where(line8 == 1 + k, -2.0 * line, near)
+            toward = jnp.where(line8 == 1 + k, line, toward)
+        near = jnp.where(line8 == 4, square, near)
+        near_ref[i] = observer_side(near, width)
+        toward_ref[i] = observer_side(toward, width)
 
     for c in range(quantities):
         plane = fields_ref[c].reshape(rows, depth)
         stacked = jnp.concatenate([plane[:, i * 128:(i + 1) * 128] for i in range(chunks)], axis=0)
         table_ref[c * 128:(c + 1) * 128, :] = two_parts(stacked.T, 1)
+
+    def prepare(m):
+        sides = panel_side(place_ref[m])
+        depth_used = sides.shape[0]
+        for i in range(own_blocks):
+            left = near_ref[i][:, :depth_used]
+            line = lines_ref[m, i:i + 1]
+            for t in range(panels // tile):
+                lanes = slice(t * tile, (t + 1) * tile)
+                square = jnp.dot(left, sides[:, lanes], preferred_element_type=jnp.float32)
+                inverse_ref[m, i, :, lanes] = lax.rsqrt(square)
+                hot_ref[m, i, :, lanes] = (
+                    lax.broadcasted_iota(jnp.int32, (bins, tile), 0) == line[:, lanes]
+                ).astype(jnp.float32).astype(jnp.bfloat16)
+
+    prepare(my_member)
+
+    pl.semaphore_wait(barrier, devices - 1)
+
+    @pl.loop(1, devices)
+    def _(k):
+        other = lax.rem(me + k, devices)
+        request_copy(other, other, me, me).start()
+
+    for copy in halo_one:
+        copy.start()
+
+    @pl.loop(1, members)
+    def _(k):
+        other = lax.rem(my_member + k, members)
+        place_copy(other, my_member).start()
+        lines_copy(other, my_member).start()
+
+    arrived_ref[me] = request_ref[me]
 
     def receive_request(s):
         @pl.when(s != me)
@@ -248,7 +344,14 @@
 
     returned_ref[me] = looked_ref[me]
 
-    for load in loads[3:]:
+    @pl.loop(1, members)
+    def _(k):
+        m = lax.rem(my_member + members - k, members)
+        place_copy(m, m).wait_recv()
+        lines_copy(m, m).wait_recv()
+        prepare(m)
+
+    for load in loads[6:]:
         load.wait()
     for copy in halo_one:
         copy.wait_recv()
@@ -268,64 +371,57 @@
         s = lax.rem(me + devices - k, devices)
         sample_copy(s, s, s).wait_recv()
 
-    weight = scale * area_ref[...]
-    for c in range(quantities):
-        got = returned_ref[:, c, :].T
-        spread = jnp.dot(
-            two_parts(got, 1), jnp.concatenate([owned_b, owned_b], axis=0),
-            preferred_element_type=jnp.float32)
-        sample = jnp.sum(spread * ranked, axis=0, keepdims=True)
-        rows_ref[c:c + 1, :] = sample * weight
-
-    home = me // per_block
-    lag = min(3, blocks)
-
-    @pl.loop(0, blocks)
-    def _(turn):
-        block = lax.rem(home + 1 + turn, blocks)
-        place = pl.multiple_of(block * width, width)
-        spots = [
-            jnp.broadcast_to(observer_ref[k:k + 1, pl.ds(place, width)], (128, width)).T
-            for k in range(3)
-        ]
-        line = bins_ref[pl.ds(block, 1), :]
-        acc = jnp.zeros((width, bins), jnp.float32)
-        for j in range(panels // tile):
-            pieces = []
-            for i in range(width // 32):
-                strip = []
-                for h in range(tile // 128):
-                    lanes = slice(j * tile + h * 128, j * tile + (h + 1) * 128)
-                    take = slice(i * 32, (i + 1) * 32)
-                    d0 = spots[0][take] - position_ref[0:1, lanes]
-                    d1 = spots[1][take] - position_ref[1:2, lanes]
-                    d2 = spots[2][take] - position_ref[2:3, lanes]
-                    inverse = lax.rsqrt(d0 * d0 + d1 * d1 + d2 * d2)
-                    along = (
-                        rows_ref[1:2, lanes] * d0
-                        + rows_ref[2:3, lanes] * d1
-                        + rows_ref[3:4, lanes] * d2
-                    )
-                    strip.append(
-                        ((rows_ref[0:1, lanes] + along * inverse) * inverse).astype(jnp.bfloat16))
-                pieces.append(jnp.concatenate(strip, axis=1))
-            emitted = jnp.concatenate(pieces, axis=0)
-            onehot = (
-                lax.broadcasted_iota(jnp.int32, (bins, tile), 0) == line[:, j * tile:(j + 1) * tile]
-            ).astype(jnp.float32).astype(jnp.bfloat16)
-            acc = acc + lax.dot_general(emitted, onehot, NT, preferred_element_type=jnp.float32)
-        for q in range(per_block):
-            total_ref[block * per_block + q] = acc[q * share:(q + 1) * share]
-        for r in range(half):
-            pair_copy(block * half + r).start()
-
-        @pl.when(turn >= lag)
-        def _():
-            merge(lax.rem(home + 1 + turn - lag + blocks, blocks))
-
-    for back in reversed(range(lag)):
-        merge(lax.rem(home - back + blocks, blocks))
-    landed_ref[mine] = merged_ref[mine]
+    got = jnp.concatenate([returned_ref[d] for d in range(devices)], axis=0)
+    spread = jnp.dot(two_parts(got, 1), ranked_ref[...], preferred_element_type=jnp.float32)
+    named = lax.broadcasted_iota(jnp.int32, (devices * quantities, panels), 0) // quantities
+    kept = jnp.where(named == owner_ref[...], spread, 0.0)
+    pair = kept[0:2 * quantities]
+    for a in range(1, devices // 2):
+        pair = pair + kept[2 * quantities * a:2 * quantities * (a + 1)]
+    weighted_ref[my_member, 0:4] = (pair[:quantities] + pair[quantities:]) * (scale * area_ref[...])
+
+    @pl.loop(1, members)
+    def _(k):
+        weighted_copy(lax.rem(my_member + k, members), my_member).start()
+
+    sum_ref[...] = jnp.zeros(sum_ref.shape, jnp.float32)
+
+    def contribute(m):
+        mine = weighted_ref[m, 0:4]
+        weighted_ref[m, 4:8] = mine * place_ref[m, 0:4]
+        sides = panel_side(weighted_ref[m])
+        depth_used = sides.shape[0]
+        for i in range(own_blocks):
+            left = toward_ref[i][:, :depth_used]
+            acc = sum_ref[i]
+            for t in range(panels // tile):
+                lanes = slice(t * tile, (t + 1) * tile)
+                along = jnp.dot(left, sides[:, lanes], preferred_element_type=jnp.float32)
+                inverse = inverse_ref[m, i, :, lanes]
+                emitted = ((mine[0:1, lanes] + along * inverse) * inverse).astype(jnp.bfloat16)
+                acc = acc + lax.dot_general(
+                    emitted, hot_ref[m, i, :, lanes], NT, preferred_element_type=jnp.float32)
+            sum_ref[i] = acc
+
+    contribute(my_member)
+
+    @pl.loop(1, members)
+    def _(k):
+        m = lax.rem(my_member + members - k, members)
+        weighted_copy(m, m).wait_recv()
+        contribute(m)
+
+    for i in range(own_blocks):
+        for k in range(per_block):
+            target = block_of(my_member, i) * per_block + k
+
+            @pl.when(target != me)
+            def _():
+                total_copy(i, k, target, my_group).start()
+
+            @pl.when(target == me)
+            def _():
+                landed_ref[my_group] = sum_ref[i, k * share:(k + 1) * share]
 
     for copy in halo_two:
         copy.wait_recv()
@@ -334,13 +430,6 @@
         advanced_ref[c, x] = 0.5 * fields_ref[c, x] + 0.5 * (center + time_step * rate)
 
     section(middle_ref, x_two_ref, y_two_ref, pad_ref, velocity_ref, diffusion_ref, keep_advanced)
-
-    @pl.loop(1, devices // 2)
-    def _(k):
-        s = lax.rem(mine + devices // 2 - k, devices // 2)
-        total_copy(s, s).wait_recv()
-
-    signal_ref[...] = jnp.sum(landed_ref[...], axis=0)
 
     @pl.loop(1, devices)
     def _(k):
@@ -348,16 +437,33 @@
         request_copy(other, other, me, me).wait_send()
         sample_copy(other, other, me).wait_send()
 
-    @pl.loop(1, devices // 2)
-    def _(k):
-        total_copy(lax.rem(mine + k, devices // 2), mine).wait_send()
-
-    @pl.loop(0, devices // 2)
-    def _(h):
-        pair_copy(h).wait_send()
+    @pl.loop(1, members)
+    def _(k):
+        other = lax.rem(my_member + k, members)
+        place_copy(other, my_member).wait_send()
+        lines_copy(other, my_member).wait_send()
+        weighted_copy(other, my_member).wait_send()
 
     for copy in halo_one + halo_two:
         copy.wait_send()
+
+    for i in range(own_blocks):
+        for k in range(per_block):
+            target = block_of(my_member, i) * per_block + k
+
+            @pl.when(target != me)
+            def _():
+                total_copy(i, k, target, my_group).wait_send()
+
+    source = member_of(me // per_block)
+
+    @pl.loop(0, groups)
+    def _(g):
+        @pl.when(jnp.logical_or(g != my_group, source != my_member))
+        def _():
+            total_copy(0, 0, lax.rem(me + 1, devices), g).wait_recv()
+
+    signal_ref[...] = jnp.sum(landed_ref[...], axis=0)
 
 
 def per_device(
@@ -369,16 +475,20 @@
     devices = grid_x * grid_y
     panels = panel_cell.shape[0]
     cap = 4 * panels // devices
+    blocks = panel_bins.shape[0]
     observers = observer_position.shape[1]
     share = observers // devices
+    width = observers // blocks
     quantities = fields.shape[0]
     scale = (bins / (panels * devices)) ** 0.5
     columns = 2 * fields.shape[1] * fields.shape[2] * fields.shape[3] // 128
+    members = 2 * grid_y
+    own_blocks = blocks // members
+    sends = own_blocks * (width // share)
 
     owner, cell, area = (
         panel_owner.reshape(1, panels), panel_cell.reshape(1, panels), panel_area.reshape(1, panels))
     vmem = pl.BlockSpec(memory_space=pltpu.VMEM)
-    smem = pl.BlockSpec(memory_space=pltpu.SMEM)
     anywhere = pl.BlockSpec(memory_space=pl.ANY)
     nx, ny, nz = fields.shape[1:]
     beside_x = pltpu.VMEM((2, quantities, 2, ny, nz), jnp.float32)
@@ -389,12 +499,15 @@
             jax.ShapeDtypeStruct(fields.shape, jnp.float32),
             jax.ShapeDtypeStruct((share, bins), jnp.float32),
         ),
-        in_specs=[anywhere] * 2 + [smem] + [anywhere] * 6,
+        in_specs=[anywhere] * 9,
         out_specs=(vmem, vmem),
         scratch_shapes=[
+            pltpu.VMEM(fields.shape, jnp.float32),
+            pltpu.VMEM(velocity.shape, jnp.float32),
+            pltpu.SMEM(diffusion.shape, jnp.float32),
+        ] + [
             pltpu.VMEM(array.shape, array.dtype)
-            for array in (
-                fields, velocity, owner, cell, panel_bins, panel_position, area, observer_position)
+            for array in (owner, cell, panel_bins, panel_position, area, observer_position)
         ] + [
             pltpu.VMEM(fields.shape, jnp.float32),
             pltpu.VMEM((quantities, nx, ny + 16, nz), jnp.float32),
@@ -404,17 +517,24 @@
             pltpu.VMEM((devices, quantities, cap), jnp.float32),
             pltpu.VMEM((devices, quantities, cap), jnp.float32),
             pltpu.VMEM((quantities * 128, columns), jnp.bfloat16),
-            pltpu.VMEM((quantities, panels), jnp.float32),
-            pltpu.VMEM((devices, share, bins), jnp.float32),
-            pltpu.VMEM((devices // 2, share, bins), jnp.float32),
-            pltpu.VMEM((devices // 2, share, bins), jnp.float32),
-            pltpu.VMEM((devices // 2, share, bins), jnp.float32),
+            pltpu.VMEM((2 * cap, panels), jnp.bfloat16),
+            pltpu.VMEM((members, 8, panels), jnp.float32),
+            pltpu.VMEM((members, own_blocks, panels), jnp.int32),
+            pltpu.VMEM((members, own_blocks, panels), jnp.int32),
+            pltpu.VMEM((members, 8, panels), jnp.float32),
+            pltpu.VMEM((own_blocks, width, 128), jnp.bfloat16),
+            pltpu.VMEM((own_blocks, width, 128), jnp.bfloat16),
+            pltpu.VMEM((members, own_blocks, width, panels), jnp.float32),
+            pltpu.VMEM((members, own_blocks, bins, panels), jnp.bfloat16),
+            pltpu.VMEM((own_blocks, width, bins), jnp.float32),
+            pltpu.VMEM((devices // members, share, bins), jnp.float32),
         ] + [
             pltpu.SemaphoreType.DMA((devices,))] * 4 + [
-            pltpu.SemaphoreType.DMA((devices // 2,))] * 2 + [
+            pltpu.SemaphoreType.DMA((sends,)),
+            pltpu.SemaphoreType.DMA((devices // members,))] + [
             pltpu.SemaphoreType.DMA((8,))] * 2 + [
-            pltpu.SemaphoreType.DMA((devices // 2,))] * 2 + [
-            pltpu.SemaphoreType.DMA((8,))],
+            pltpu.SemaphoreType.DMA((members,))] * 6 + [
+            pltpu.SemaphoreType.DMA((9,))],
         compiler_params=pltpu.CompilerParams(
             collective_id=0, has_side_effects=True),
         cost_estimate=pl.CostEstimate(

time: 43 us -> 36.9 us (0.86)
  the two profiles are of different devices: /device:TPU:15 before, /device:TPU:0 now
where the time goes in v1:
time: 36.9 us; the launch traced here: 36.2 us
  Pallas kernels  33.3 us (90%)
  local copies, waits for them, and re-layouts  2.3 us (6%)
  between operations  0.65 us (2%)
    pallas_call x1, Pallas kernels, per_device(): pl.pallas_call(functools.partial(emission_kernel, grid_x, grid_y, cap, sc...  33.3 us
    unnamed x4, local copies, waits for them, and re-layouts  2.3 us

profile of v1, /device:TPU:0, one launch (start us, length us, event | category | flops | bytes accessed | tf_op | source)
XLA Modules:
  0.0 36.2 jit_solution(14763077558317395369)
XLA Ops:
  0.6 33.3 %shard_map.104 = (f32[4,4,8,512]{3,2,1,0:T(8,128)}, f32[64,128]{1,0:T(8,128)}) custom-call(f32[4,4,8,512]{3,2,1,0:T(8,128)} %fields_in.1, f32[3,4,8,512]{3,2,1,0:T(8,128)} %velocity_in.1, f32[4]{0:T(128)} %diffusion_in.1, s32[1,1024]{1,0:T(1,128)} %bitcast.3, s32[1,1024]{1,0:T(1,128)} %bitcast.4, s32[16,1024]{1,0:T(8,128)} %bins_in.1, ...), custom_call_target="tpu_custom_call" | custom-call | flops 40000000000 | bytes 4000000 | tf_op jit(solution)/shard_map/pallas_call | solution.py:496
  33.9 0.0 copy-start
  33.9 1.7 %copy.13 = f32[4,4,8,512]{3,2,1,0:T(8,128)} copy(f32[4,4,8,512]{3,2,1,0:T(8,128)} %get-tuple-element.4) | data formatting | bytes 524288
  35.6 0.0 copy-done
  35.6 0.6 %copy.14 = f32[64,128]{1,0:T(8,128)} copy(f32[64,128]{1,0:T(8,128)S(1)} %copy-done) | data formatting | bytes 65536
Async XLA Ops:
  33.9 1.7 %copy-start = (f32[64,128]{1,0:T(8,128)S(1)}, f32[64,128]{1,0:T(8,128)}, u32[]{:S(2)}) copy-start(f32[64,128]{1,0:T(8,128)} %get-tuple-element.5) | copy-start | bytes 98308

commit v2 on v1

--- a/solution.py
+++ b/solution.py
@@ -128,12 +128,26 @@
         core = block // (across * own_blocks * 2)
         return bit * grid_y + y * 2 + core
 
+    device_bits = [1 << b for b in range((devices - 1).bit_length())]
+    device_steps = [bit * (1 - 2 * lax.rem(me // bit, 2)) for bit in device_bits]
+
+    def peer(k):
+        return me + sum(step for bit, step in zip(device_bits, device_steps) if k & bit)
+
+    def flipped(base, k, bits):
+        for bit in bits:
+            base = base + bit * lax.rem(k // bit, 2) * (1 - 2 * lax.rem(base // bit, 2))
+        return base
+
+    member_bits = [1 << b for b in range((members - 1).bit_length())]
+
+    def mate(k):
+        return flipped(my_member, k, member_bits)
+
     barrier = pltpu.get_barrier_semaphore()
 
-    @pl.loop(1, devices)
-    def _(k):
-        pl.semaphore_signal(
-            barrier, inc=1, device_id=at(lax.rem(me + k, devices)), device_id_type=MESH)
+    for k in reversed(range(1, devices)):
+        pl.semaphore_signal(barrier, inc=1, device_id=at(peer(k)), device_id_type=MESH)
 
     loads = [
         pltpu.make_async_copy(source, target, load_sem.at[i])
@@ -287,69 +301,78 @@
 
     pl.semaphore_wait(barrier, devices - 1)
 
-    @pl.loop(1, devices)
+    for k in reversed(range(1, devices)):
+        other = peer(k)
+        request_copy(other, other, me, me).start()
+
+    @pl.loop(1, members)
     def _(k):
-        other = lax.rem(me + k, devices)
-        request_copy(other, other, me, me).start()
+        other = mate(k)
+        place_copy(other, my_member).start()
+        lines_copy(other, my_member).start()
 
     for copy in halo_one:
         copy.start()
 
-    @pl.loop(1, members)
-    def _(k):
-        other = lax.rem(my_member + k, members)
-        place_copy(other, my_member).start()
-        lines_copy(other, my_member).start()
-
     arrived_ref[me] = request_ref[me]
+
+    def prepare_mates(first, last):
+        @pl.loop(first, last)
+        def _(k):
+            m = mate(k)
+            place_copy(m, m).wait_recv()
+            lines_copy(m, m).wait_recv()
+            prepare(m)
+
+    early = members // 2
+    prepare_mates(1, early)
 
     def receive_request(s):
         @pl.when(s != me)
         def _():
             request_copy(s, s, me, s).wait_recv()
 
-    @pl.loop(0, devices // 2)
-    def _(pair):
-        first = lax.rem(me + devices - 2 * pair, devices)
-        second = lax.rem(me + devices - 2 * pair - 1, devices)
-        receive_request(first)
-        receive_request(second)
-        asked = jnp.concatenate([arrived_ref[first], arrived_ref[second]], axis=1)
+    batch = min(8, devices)
+
+    @pl.loop(0, devices // batch)
+    def _(turn):
+        base = flipped(me, turn * batch, device_bits)
+        sources = [flipped(base, k, device_bits) for k in range(batch)]
+        for s in sources:
+            receive_request(s)
+        asked = jnp.concatenate([arrived_ref[s] for s in sources], axis=1)
         low = lax.bitwise_and(asked, 127)
         line = lax.shift_right_logical(asked, row_shift)
         chunk = lax.bitwise_and(lax.shift_right_logical(asked, 7), chunks - 1)
         high = chunk * rows + line
-        pick = (
-            lax.broadcasted_iota(jnp.int32, (chunks * rows, 2 * cap), 0) == high
-        ).astype(jnp.float32).astype(jnp.bfloat16)
-        found = jnp.dot(
-            table_ref[...], jnp.concatenate([pick, pick], axis=0),
-            preferred_element_type=jnp.float32)
-        lane = lax.broadcasted_iota(jnp.int32, (128, 2 * cap), 0) == low
-        values = jnp.concatenate(
-            [
-                jnp.sum(jnp.where(lane, found[c * 128:(c + 1) * 128], 0.0), axis=0, keepdims=True)
-                for c in range(quantities)
-            ],
-            axis=0,
-        )
-        looked_ref[first] = values[:, :cap]
-        looked_ref[second] = values[:, cap:]
-
-        @pl.when(first != me)
-        def _():
-            sample_copy(first, first, me).start()
-
-        sample_copy(second, second, me).start()
+        span = batch * cap
+        step = min(256, span)
+        for first in range(0, span, step):
+            part = slice(first, first + step)
+            pick = (
+                lax.broadcasted_iota(jnp.int32, (chunks * rows, step), 0) == high[:, part]
+            ).astype(jnp.float32).astype(jnp.bfloat16)
+            found = jnp.dot(
+                table_ref[...], jnp.concatenate([pick, pick], axis=0),
+                preferred_element_type=jnp.float32)
+            lane = lax.broadcasted_iota(jnp.int32, (128, step), 0) == low[:, part]
+            values = jnp.concatenate(
+                [
+                    jnp.sum(
+                        jnp.where(lane, found[c * 128:(c + 1) * 128], 0.0), axis=0, keepdims=True)
+                    for c in range(quantities)
+                ],
+                axis=0,
+            )
+            for k in range(step // cap):
+                looked_ref[sources[first // cap + k]] = values[:, k * cap:(k + 1) * cap]
+
+        for s in sources:
+            @pl.when(s != me)
+            def _():
+                sample_copy(s, s, me).start()
 
     returned_ref[me] = looked_ref[me]
-
-    @pl.loop(1, members)
-    def _(k):
-        m = lax.rem(my_member + members - k, members)
-        place_copy(m, m).wait_recv()
-        lines_copy(m, m).wait_recv()
-        prepare(m)
 
     for load in loads[6:]:
         load.wait()
@@ -365,6 +388,8 @@
     section(fields_ref, x_one_ref, y_one_ref, pad_ref, velocity_ref, diffusion_ref, keep_middle)
     for copy in halo_two:
         copy.start()
+
+    prepare_mates(early, members)
 
     @pl.loop(1, devices)
     def _(k):
@@ -382,7 +407,7 @@
 
     @pl.loop(1, members)
     def _(k):
-        weighted_copy(lax.rem(my_member + k, members), my_member).start()
+        weighted_copy(mate(members - k), my_member).start()
 
     sum_ref[...] = jnp.zeros(sum_ref.shape, jnp.float32)
 
@@ -407,7 +432,7 @@
 
     @pl.loop(1, members)
     def _(k):
-        m = lax.rem(my_member + members - k, members)
+        m = mate(k)
         weighted_copy(m, m).wait_recv()
         contribute(m)
 
@@ -439,7 +464,7 @@
 
     @pl.loop(1, members)
     def _(k):
-        other = lax.rem(my_member + k, members)
+        other = mate(k)
         place_copy(other, my_member).wait_send()
         lines_copy(other, my_member).wait_send()
         weighted_copy(other, my_member).wait_send()
@@ -464,6 +489,17 @@
             total_copy(0, 0, lax.rem(me + 1, devices), g).wait_recv()
 
     signal_ref[...] = jnp.sum(landed_ref[...], axis=0)
+
+
+def write_kernel(advanced_in, signal_in, advanced_out, signal_out, sems):
+    copies = [
+        pltpu.make_async_copy(advanced_in, advanced_out, sems.at[0]),
+        pltpu.make_async_copy(signal_in, signal_out, sems.at[1]),
+    ]
+    for copy in copies:
+        copy.start()
+    for copy in copies:
+        copy.wait()
 
 
 def per_device(
@@ -490,16 +526,17 @@
         panel_owner.reshape(1, panels), panel_cell.reshape(1, panels), panel_area.reshape(1, panels))
     vmem = pl.BlockSpec(memory_space=pltpu.VMEM)
     anywhere = pl.BlockSpec(memory_space=pl.ANY)
+    outside = pl.BlockSpec(memory_space=pltpu.HBM)
     nx, ny, nz = fields.shape[1:]
     beside_x = pltpu.VMEM((2, quantities, 2, ny, nz), jnp.float32)
     beside_y = pltpu.VMEM((2, quantities, nx, 2, nz), jnp.float32)
-    return pl.pallas_call(
+    held = pl.pallas_call(
         functools.partial(emission_kernel, grid_x, grid_y, cap, scale, min(256, panels)),
         out_shape=(
-            jax.ShapeDtypeStruct(fields.shape, jnp.float32),
-            jax.ShapeDtypeStruct((share, bins), jnp.float32),
+            pltpu.VMEM(fields.shape, jnp.float32),
+            pltpu.VMEM((share, bins), jnp.float32),
         ),
-        in_specs=[anywhere] * 9,
+        in_specs=[outside] * 9,
         out_specs=(vmem, vmem),
         scratch_shapes=[
             pltpu.VMEM(fields.shape, jnp.float32),
@@ -540,6 +577,17 @@
         cost_estimate=pl.CostEstimate(
             flops=40 * 10**9, bytes_accessed=4 * 10**6, transcendentals=2 * 10**6),
     )(fields, velocity, diffusion, owner, cell, panel_bins, panel_position, area, observer_position)
+    return pl.pallas_call(
+        write_kernel,
+        out_shape=(
+            jax.ShapeDtypeStruct(fields.shape, jnp.float32),
+            jax.ShapeDtypeStruct((share, bins), jnp.float32),
+        ),
+        in_specs=[anywhere, anywhere],
+        out_specs=(outside, outside),
+        scratch_shapes=[pltpu.SemaphoreType.DMA((2,))],
+        compiler_params=pltpu.CompilerParams(vmem_limit_bytes=2**20),
+    )(*held)
 
 
 def solution(mesh):

time: 36.9 us -> 32.2 us (0.87); the launches traced: 36.2 us -> 32 us
  local copies, waits for them, and re-layouts: 2.3 us -> 0 us
  Pallas kernels: 33.3 us -> 31.3 us
    pallas_call x1, Pallas kernels: 33.3 us -> 30.6 us  [per_device(): pl.pallas_call(functools.partial(emission_kernel, grid_x, grid_y, cap, sc...]
    unnamed x4 -> x0, local copies, waits for them, and re-layouts: 2.3 us -> none
    pallas_call x0 -> x1, Pallas kernels: none -> 0.72 us  [per_device(): pl.pallas_call(write_kernel, out_shape=(jax.ShapeDtypeStruct(fields.shape...]
where the time goes in v2:
time: 32.2 us; the launch traced here: 32 us
  Pallas kernels  31.3 us (97%)
  between operations  0.64 us (2%)
    pallas_call x1, Pallas kernels, per_device(): pl.pallas_call(functools.partial(emission_kernel, grid_x, grid_y, cap, sc...  30.6 us
    pallas_call x1, Pallas kernels, per_device(): pl.pallas_call(write_kernel, out_shape=(jax.ShapeDtypeStruct(fields.shape...  0.72 us

profile of v2, /device:TPU:0, one launch (start us, length us, event | category | flops | bytes accessed | tf_op | source)
XLA Modules:
  0.0 32.0 jit_solution(17509609503407244170)
XLA Ops:
  0.6 30.6 %shard_map.104 = (f32[4,4,8,512]{3,2,1,0:T(8,128)S(1)}, f32[64,128]{1,0:T(8,128)S(1)}) custom-call(f32[4,4,8,512]{3,2,1,0:T(8,128)} %fields_in.1, f32[3,4,8,512]{3,2,1,0:T(8,128)} %velocity_in.1, f32[4]{0:T(128)} %diffusion_in.1, s32[1,1024]{1,0:T(1,128)} %bitcast.3, s32[1,1024]{1,0:T(1,128)} %bitcast.4, s32[16,1024]{1,0:T(8,128)} %bins_in.1, ...), custom_call_target="tpu_custom_call" | custom-call | flops 40000000000 | bytes 4000000 | tf_op jit(solution)/shard_map/pallas_call | solution.py:533
  31.3 0.7 %shard_map.105 = (f32[4,4,8,512]{3,2,1,0:T(8,128)}, f32[64,128]{1,0:T(8,128)}) custom-call(f32[4,4,8,512]{3,2,1,0:T(8,128)S(1)} %get-tuple-element.4.advanced_in, f32[64,128]{1,0:T(8,128)S(1)} %get-tuple-element.5.signal_in), custom_call_target="tpu_custom_call" | custom-call | tf_op jit(solution)/shard_map/pallas_call | solution.py:580
